TPU v7x, 32 devices: a whole 2x2x4 slice. The times are simulated.
32 devices in a mesh: grp: 2 (over y), tok: 4 (over z), sec: 2 (over core), ch: 2 (over x).
Axes of the slice: x: 2, y: 2, z: 4, core: 2. Of those that a mesh axis runs over, the one named last changes fastest.
Arguments:
- features: bfloat16 [4096, 2048], P('ch', ('grp', 'tok', 'sec')), parts along dimension 1, may hold values from -6 to 6
- gate_one: bfloat16 [4096, 2048], P('ch', ('grp', 'tok', 'sec')), parts along dimension 1, may hold values from -6 to 6
- taps_one: bfloat16 [4096, 128], P('ch'), may hold values from -0.5 to 0.5
- long_filter: bfloat16 [4096, 1024], P('ch', ('tok', 'sec')), may hold values from -0.1875 to 0.1875
- skip_gain: float32 [4096], P('ch'), may hold values from 0.5 to 1.5
- taps_two: bfloat16 [4096, 128], P('ch'), may hold values from -0.5 to 0.5
- gate_two: bfloat16 [4096, 2048], P('ch', ('grp', 'tok', 'sec')), parts along dimension 1, may hold values from -6 to 6
Outputs:
- mixed_out: bfloat16 [4096, 2048], P('ch', ('grp', 'tok', 'sec')), parts along dimension 1
There are 2 independent parts, one for each index of `grp`. A program takes and returns all parts, laid end to end along the dimension named above; an argument that names none is the same for every part. Nothing has to cross between parts.
All inputs are finite; a program needn't handle non-finite values.
Results may differ from a plain program's by a relative error of at most 0.0057.
Values may be sent and summed in bfloat16 or wider, within the bound.
No kernel may reach another device: no remote copies, remote signals or barrier semaphores. Data moves between devices by JAX's collectives and lax.ppermute only.
A program may use at most 192 MiB of HBM per device.

v0:
```python
import math
import jax
import jax.numpy as jnp
from jax import lax
from jax.sharding import PartitionSpec as P


def passed_along(array, axis, by):
    length = lax.axis_size(axis)
    pairs = [(i, i + by) for i in range(length) if 0 <= i + by < length]
    return lax.ppermute(array, axis, pairs)


def depthwise(padded, kernel_taps):
    tap_count = kernel_taps.shape[1]
    length = padded.shape[1] - (tap_count - 1)
    group_size = 16
    total = jnp.zeros((padded.shape[0], length), jnp.float32)
    for first in range(0, tap_count, group_size):
        last = min(first + group_size, tap_count)
        stacked = jnp.stack(
            [padded[:, tap_count - 1 - k : tap_count - 1 - k + length] for k in range(first, last)],
            axis=1,
        )
        total = total + jnp.einsum(
            "cgl,cg->cl", stacked, kernel_taps[:, first:last], preferred_element_type=jnp.float32
        )
    return total


def angle_table(rows_count, cols_count, period):
    row_index = jnp.arange(rows_count, dtype=jnp.int32)[:, None]
    col_index = jnp.arange(cols_count, dtype=jnp.int32)[None, :]
    phase = (row_index * col_index % period).astype(jnp.float32) * (2.0 * math.pi / period)
    return (jnp.cos(phase), jnp.sin(phase))


def contract(form, left, right):
    return jnp.einsum(form, left, right, precision=lax.Precision.HIGHEST)


def forward_spectrum(signal, outer, inner, total):
    half_outer = outer // 2
    cos_first, sin_first = angle_table(half_outer, outer, outer)
    turn_cos, turn_sin = angle_table(outer, inner, total)
    cos_inner, sin_inner = angle_table(inner, inner, inner)
    shaped = signal.reshape(signal.shape[0], half_outer, inner)
    real_a = contract("cmn,mk->ckn", shaped, cos_first)
    imag_a = -contract("cmn,mk->ckn", shaped, sin_first)
    real_b = real_a * turn_cos + imag_a * turn_sin
    imag_b = imag_a * turn_cos - real_a * turn_sin
    real_c = contract("ckn,nj->cjk", real_b, cos_inner) + contract("ckn,nj->cjk", imag_b, sin_inner)
    imag_c = contract("ckn,nj->cjk", imag_b, cos_inner) - contract("ckn,nj->cjk", real_b, sin_inner)
    return (real_c, imag_c)


def inverse_spectrum(real_y, imag_y, outer, inner, total):
    half_outer = outer // 2
    cos_inner, sin_inner = angle_table(inner, inner, inner)
    turn_cos, turn_sin = angle_table(outer, inner, total)
    cos_last, sin_last = angle_table(outer, half_outer, outer)
    real_c = contract("cjk,jn->ckn", real_y, cos_inner) - contract("cjk,jn->ckn", imag_y, sin_inner)
    imag_c = contract("cjk,jn->ckn", imag_y, cos_inner) + contract("cjk,jn->ckn", real_y, sin_inner)
    real_d = real_c * turn_cos - imag_c * turn_sin
    imag_d = imag_c * turn_cos + real_c * turn_sin
    result = contract("ckn,km->cmn", real_d, cos_last) - contract("ckn,km->cmn", imag_d, sin_last)
    return (result / total).reshape(real_y.shape[0], half_outer * inner)


def on_device(features, gate_one, taps_one, long_filter, skip_gain, taps_two, gate_two):
    shards = lax.axis_size(("tok", "sec"))
    channels, block_len = features.shape
    narrow = channels // shards
    seq_len = block_len * shards
    rim_width = taps_one.shape[1] - 1
    total = 2 * seq_len
    inner = math.gcd(seq_len, 128)
    outer = total // inner
    filter_rows = lax.all_to_all(
        long_filter[:, None, :], ("tok", "sec"), split_axis=0, concat_axis=1, tiled=True
    ).reshape(narrow, seq_len)
    rim_rows = passed_along(features[:, block_len - rim_width :], ("tok", "sec"), 1)
    first_conv = depthwise(jnp.concatenate([rim_rows, features], axis=1), taps_one)
    mixed_one = (first_conv * gate_one).astype(jnp.bfloat16)
    channel_rows = lax.all_to_all(
        mixed_one[:, None, :], ("tok", "sec"), split_axis=0, concat_axis=1, tiled=True
    )
    channel_rows = channel_rows.reshape(narrow, seq_len).astype(jnp.float32)
    filter_real, filter_imag = forward_spectrum(
        filter_rows.astype(jnp.float32), outer, inner, total
    )
    signal_real, signal_imag = forward_spectrum(channel_rows, outer, inner, total)
    product_real = signal_real * filter_real - signal_imag * filter_imag
    product_imag = signal_real * filter_imag + signal_imag * filter_real
    conv_rows = inverse_spectrum(product_real, product_imag, outer, inner, total)
    skip_local = lax.dynamic_slice_in_dim(
        skip_gain, lax.axis_index(("tok", "sec")) * narrow, narrow
    )
    long_out = (conv_rows + skip_local[:, None] * channel_rows).astype(jnp.bfloat16)
    long_blocks = long_out.reshape(narrow, shards, block_len)
    tail_rows = jnp.concatenate(
        [
            jnp.zeros((narrow, 1, rim_width), jnp.bfloat16),
            long_blocks[:, :-1, block_len - rim_width :],
        ],
        axis=1,
    )
    windows = jnp.concatenate([tail_rows, long_blocks], axis=2)
    padded = lax.all_to_all(
        windows, ("tok", "sec"), split_axis=1, concat_axis=0, tiled=True
    ).reshape(channels, block_len + rim_width)
    second_conv = depthwise(padded, taps_two)
    return (second_conv * gate_two).astype(jnp.bfloat16)


def solution(mesh):
    in_specs = (
        P("ch", ("grp", "tok", "sec")),
        P("ch", ("grp", "tok", "sec")),
        P("ch", None),
        P("ch", ("tok", "sec")),
        P("ch"),
        P("ch", None),
        P("ch", ("grp", "tok", "sec")),
    )
    out_specs = P("ch", ("grp", "tok", "sec"))
    return jax.shard_map(
        on_device, mesh=mesh, in_specs=in_specs, out_specs=out_specs, check_vma=False
    )
```

profile of v0, /device:TPU:0, one launch (start us, length us, event | category | flops | bytes accessed | tf_op | source)
XLA Modules:
  0.0 428.6 jit_solution(18028862349489927458)
XLA Ops:
  8.2 6.1 %all-to-all-start.1 = ((bf16[8,2,16384]{2,1,0:T(2,128)(2,1)}), bf16[8,2,16384]{2,1,0:T(2,128)(2,1)S(1)}, u32[]{:S(2)}, u32[]{:S(2)}) async-start(bf16[8,2,16384]{2,1,0:T(2,128)(2,1)} %reshape.112), calls=%async_computation.1 | async-start | bytes 1048576 | tf_op jit(solution)/shard_map/all_to_all | solution.py:79
  14.3 5.7 %slice_bitcast_fusion.142 = (bf16[2048,16,1]{1,0,2:T(8,128)(2,1)S(1)}, bf16[2048,16,1]{1,0,2:T(8,128)(2,1)}, bf16[2048,16,1]{1,0,2:T(8,128)(2,1)}, bf16[2048,16,...) fusion(bf16[2048,128]{1,0:T(8,128)(2,1)} %param.9), kind=kLoop, calls=%fused_computation.1013 | loop fusion | bytes 1048576 | tf_op jit(solution)/shard_map/slice | solution.py:26
  28.0 3.2 copy-done.13
  31.2 3.7 constant_dynamic-update-slice_fusion.16
  50.8 3.0 constant_dynamic-update-slice_fusion
  60.1 3.2 constant_dynamic-update-slice_fusion.32
  69.1 2.8 constant_dynamic-update-slice_fusion.48
  110.7 8.7 %fusion.16 = f32[2048,1,128]{2,1,0:T(1,128)S(1)} fusion(bf16[2048,16,128]{2,0,1:T(8,128)(2,1)} %constant_dynamic-update-slice_fusion.112, bf16[2048,16,1]{1,0,2:T(8,128)(2,1)S(1)} %get-tuple-element.191), kind=kOutput, calls=%fused_computation.268 | convolution fusion | flops 8388608 | bytes 9502720 | tf_op jit(solution)/shard_map/cgl,cg->cl/dot_general | solution.py:25
  119.4 8.7 %fusion.18 = f32[2048,1,128]{2,1,0:T(1,128)S(1)} fusion(bf16[2048,16,128]{2,0,1:T(8,128)(2,1)} %get-tuple-element.175, bf16[2048,16,1]{1,0,2:T(8,128)(2,1)S(1)} %get-tuple-element.192), kind=kOutput, calls=%fused_computation.270 | convolution fusion | flops 8388608 | bytes 9502720 | tf_op jit(solution)/shard_map/cgl,cg->cl/dot_general | solution.py:25
  128.2 9.0 %fusion.20 = f32[2048,1,128]{2,1,0:T(1,128)S(1)} fusion(bf16[2048,16,128]{2,0,1:T(8,128)(2,1)} %copy-done.9, bf16[2048,16,1]{1,0,2:T(8,128)(2,1)} %get-tuple-element.186), kind=kOutput, calls=%fused_computation.272 | convolution fusion | flops 8388608 | bytes 9502720 | tf_op jit(solution)/shard_map/cgl,cg->cl/dot_general | solution.py:25
  137.1 9.8 %fusion.22 = f32[2048,1,128]{2,1,0:T(1,128)} fusion(bf16[2048,16,128]{2,0,1:T(8,128)(2,1)} %copy-done.8, bf16[2048,16,1]{1,0,2:T(8,128)(2,1)} %get-tuple-element.187), kind=kOutput, calls=%fused_computation.274 | convolution fusion | flops 8388608 | bytes 9502720 | tf_op jit(solution)/shard_map/cgl,cg->cl/dot_general | solution.py:25
  146.9 10.2 %fusion.24 = f32[2048,1,128]{2,1,0:T(1,128)} fusion(bf16[2048,16,128]{2,0,1:T(8,128)(2,1)} %copy-done.7, bf16[2048,16,1]{1,0,2:T(8,128)(2,1)} %get-tuple-element.188), kind=kOutput, calls=%fused_computation.276 | convolution fusion | flops 8388608 | bytes 9502720 | tf_op jit(solution)/shard_map/cgl,cg->cl/dot_general | solution.py:25
  157.1 9.8 %fusion.26 = f32[2048,1,128]{2,1,0:T(1,128)} fusion(bf16[2048,16,128]{2,0,1:T(8,128)(2,1)} %copy-done.6, bf16[2048,16,1]{1,0,2:T(8,128)(2,1)} %get-tuple-element.189), kind=kOutput, calls=%fused_computation.278 | convolution fusion | flops 8388608 | bytes 9502720 | tf_op jit(solution)/shard_map/cgl,cg->cl/dot_general | solution.py:25
  166.8 9.9 %fusion.30 = f32[2048,1,128]{2,1,0:T(1,128)} fusion(bf16[2048,16,128]{2,0,1:T(8,128)(2,1)} %get-tuple-element.149, bf16[2048,16,1]{1,0,2:T(8,128)(2,1)S(1)} %get-tuple-element.190), kind=kOutput, calls=%fused_computation.282 | convolution fusion | flops 8388608 | bytes 9502720 | tf_op jit(solution)/shard_map/cgl,cg->cl/dot_general | solution.py:25
  176.7 9.8 %fusion.28 = f32[2048,1,128]{2,1,0:T(1,128)} fusion(bf16[2048,16,128]{2,0,1:T(8,128)(2,1)} %get-tuple-element.141, bf16[2048,16,1]{1,0,2:T(8,128)(2,1)S(1)} %get-tuple-element.185), kind=kOutput, calls=%fused_computation.280 | convolution fusion | flops 8388608 | bytes 9502720 | tf_op jit(solution)/shard_map/cgl,cg->cl/dot_general | solution.py:25
  186.5 2.9 fusion.111
  191.4 5.1 %all-to-all-start = ((bf16[8,2,16384]{2,1,0:T(2,128)(2,1)}), bf16[8,2,16384]{2,1,0:T(2,128)(2,1)}, u32[]{:S(2)}, u32[]{:S(2)}) async-start(bf16[8,2,16384]{2,1,0:T(2,128)(2,1)} %reshape.110), calls=%async_computation | async-start | bytes 1048576 | tf_op jit(solution)/shard_map/all_to_all | solution.py:85
  199.1 2.4 fusion.367
  201.5 10.4 %all-to-all-done = bf16[8,2,16384]{2,1,0:T(2,128)(2,1)} async-done(((bf16[8,2,16384]{2,1,0:T(2,128)(2,1)}), bf16[8,2,16384]{2,1,0:T(2,128)(2,1)}, u32[]{:S(2)}, u32[]{:S(2)}) %all-to-all-start) | async-done | bytes 524320 | tf_op jit(solution)/shard_map/all_to_all | solution.py:85
  211.9 2.6 reshape.111
  215.7 3.5 add_bitcast_fusion
  219.3 2.6 fusion.47
  221.9 2.6 fusion.45
  224.5 2.6 fusion.55
  227.1 2.7 fusion.53
  229.9 2.7 fusion.67
  232.6 2.7 fusion.70
  235.3 2.7 fusion.61
  238.0 3.3 multiply_subtract_fusion.1
  241.3 3.6 fusion.34
  244.9 3.6 fusion.32
  248.6 4.0 fusion.73
  252.5 3.8 multiply_subtract_fusion
  258.6 2.6 fusion.91
  263.2 3.7 all-to-all-start.2
  266.9 2.7 slice_bitcast_fusion.134
  269.6 23.6 %all-to-all-done.2 = bf16[256,8,255]{2,0,1:T(8,128)(2,1)S(1)} async-done(((bf16[256,8,255]{2,0,1:T(8,128)(2,1)}), bf16[256,8,255]{2,0,1:T(8,128)(2,1)S(1)}, u32[]{:S(2)}, u32[]{:S(2)}) %all-to-all-start.2) | async-done | bytes 1044512 | tf_op jit(solution)/shard_map/all_to_all | solution.py:109
  293.3 2.8 constant_dynamic-update-slice_fusion.159
  296.0 3.0 constant_dynamic-update-slice_fusion.158
  299.1 3.0 constant_dynamic-update-slice_fusion.157
  302.1 3.0 constant_dynamic-update-slice_fusion.156
  305.1 3.0 constant_dynamic-update-slice_fusion.155
  308.1 3.1 constant_dynamic-update-slice_fusion.154
  311.2 3.0 constant_dynamic-update-slice_fusion.153
  314.1 3.0 constant_dynamic-update-slice_fusion.152
  317.2 3.1 constant_dynamic-update-slice_fusion.151
  320.2 3.2 constant_dynamic-update-slice_fusion.150
  323.4 3.0 constant_dynamic-update-slice_fusion.149
  326.4 3.1 constant_dynamic-update-slice_fusion.148
  329.5 3.0 constant_dynamic-update-slice_fusion.147
  332.5 3.0 constant_dynamic-update-slice_fusion.146
  335.5 3.0 constant_dynamic-update-slice_fusion.145
  338.5 2.8 constant_dynamic-update-slice_fusion.144
  341.4 3.2 copy-done.10
  344.6 2.6 copy-done.11
  349.6 9.1 %fusion.14 = f32[2048,1,128]{2,1,0:T(1,128)S(1)} fusion(bf16[2048,16,128]{2,0,1:T(8,128)(2,1)} %get-tuple-element.20, bf16[2048,16,1]{1,0,2:T(8,128)(2,1)S(1)} %copy-done.5), kind=kOutput, calls=%fused_computation.266 | convolution fusion | flops 8388608 | bytes 9502720 | tf_op jit(solution)/shard_map/cgl,cg->cl/dot_general | solution.py:25
  358.7 8.7 %fusion.12 = f32[2048,1,128]{2,1,0:T(1,128)S(1)} fusion(bf16[2048,16,128]{2,0,1:T(8,128)(2,1)} %copy-done.10, bf16[2048,16,1]{1,0,2:T(8,128)(2,1)S(1)} %copy-done.4), kind=kOutput, calls=%fused_computation.264 | convolution fusion | flops 8388608 | bytes 9502720 | tf_op jit(solution)/shard_map/cgl,cg->cl/dot_general | solution.py:25
  367.5 8.9 %fusion.10 = f32[2048,1,128]{2,1,0:T(1,128)S(1)} fusion(bf16[2048,16,128]{2,0,1:T(8,128)(2,1)} %get-tuple-element.19, bf16[2048,16,1]{1,0,2:T(8,128)(2,1)S(1)} %get-tuple-element.181), kind=kOutput, calls=%fused_computation.262 | convolution fusion | flops 8388608 | bytes 9502720 | tf_op jit(solution)/shard_map/cgl,cg->cl/dot_general | solution.py:25
  376.4 8.8 %fusion.8 = f32[2048,1,128]{2,1,0:T(1,128)S(1)} fusion(bf16[2048,16,128]{2,0,1:T(8,128)(2,1)} %get-tuple-element.18, bf16[2048,16,1]{1,0,2:T(8,128)(2,1)} %get-tuple-element.180), kind=kOutput, calls=%fused_computation.260 | convolution fusion | flops 8388608 | bytes 9502720 | tf_op jit(solution)/shard_map/cgl,cg->cl/dot_general | solution.py:25
  385.1 9.9 %fusion.6 = f32[2048,1,128]{2,1,0:T(1,128)} fusion(bf16[2048,16,128]{2,0,1:T(8,128)(2,1)} %get-tuple-element.17, bf16[2048,16,1]{1,0,2:T(8,128)(2,1)} %get-tuple-element.179), kind=kOutput, calls=%fused_computation.258 | convolution fusion | flops 8388608 | bytes 9502720 | tf_op jit(solution)/shard_map/cgl,cg->cl/dot_general | solution.py:25
  395.0 9.8 %fusion.4 = f32[2048,1,128]{2,1,0:T(1,128)} fusion(bf16[2048,16,128]{2,0,1:T(8,128)(2,1)} %get-tuple-element.16, bf16[2048,16,1]{1,0,2:T(8,128)(2,1)} %get-tuple-element.178), kind=kOutput, calls=%fused_computation.256 | convolution fusion | flops 8388608 | bytes 9502720 | tf_op jit(solution)/shard_map/cgl,cg->cl/dot_general | solution.py:25
  404.8 9.7 %fusion.2 = f32[2048,1,128]{2,1,0:T(1,128)} fusion(bf16[2048,16,128]{2,0,1:T(8,128)(2,1)} %copy-done.12, bf16[2048,16,1]{1,0,2:T(8,128)(2,1)S(1)} %get-tuple-element.184), kind=kOutput, calls=%fused_computation.254 | convolution fusion | flops 8388608 | bytes 9502720 | tf_op jit(solution)/shard_map/cgl,cg->cl/dot_general | solution.py:25
  414.5 10.1 %fusion = f32[2048,1,128]{2,1,0:T(1,128)} fusion(bf16[2048,16,128]{2,0,1:T(8,128)(2,1)} %copy-done.11, bf16[2048,16,1]{1,0,2:T(8,128)(2,1)} %get-tuple-element.183), kind=kOutput, calls=%fused_computation.252 | convolution fusion | flops 8388608 | bytes 9502720 | tf_op jit(solution)/shard_map/cgl,cg->cl/dot_general | solution.py:25
  424.5 3.6 multiply_convert_fusion
  (140 shorter events, 95.1 us)
Async XLA Ops:
  0.0 20.0 %copy-start = (bf16[2048,128]{1,0:T(8,128)(2,1)S(1)}, bf16[2048,128]{1,0:T(8,128)(2,1)}, u32[]{:S(2)}) copy-start(bf16[2048,128]{1,0:T(8,128)(2,1)} %param.7) | copy-start | bytes 1572868
  2.1 17.9 %collective-permute-start = (bf16[2048,127]{1,0:T(8,128)(2,1)}, bf16[2048,127]{1,0:T(8,128)(2,1)S(1)}, u32[]{:S(2)}, u32[]{:S(2)}) collective-permute-start(bf16[2048,127]{1,0:T(8,128)(2,1)} %slice.819), channel_id=1, source_target_pairs={{0,2},{2,4},{4,6},{6,8},{8,10},{10,12},{12,14},{1,3},{3,5},{5,7},{... | collective-permute-start | bytes 1560584 | tf_op jit(solution)/shard_map/ppermute | solution.py:11
  8.2 183.2 %all-to-all-start.1 = ((bf16[8,2,16384]{2,1,0:T(2,128)(2,1)}), bf16[8,2,16384]{2,1,0:T(2,128)(2,1)S(1)}, u32[]{:S(2)}, u32[]{:S(2)}) async-start(bf16[8,2,16384]{2,1,0:T(2,128)(2,1)} %reshape.112), calls=%async_computation.1 | async-start | bytes 1048576 | tf_op jit(solution)/shard_map/all_to_all | solution.py:79
  28.0 3.2 copy-start.13
  63.3 5.3 %copy-start.6 = (bf16[2048,16,128]{2,0,1:T(8,128)(2,1)}, bf16[2048,16,128]{2,0,1:T(8,128)(2,1)S(1)}, u32[]{:S(2)}) copy-start(bf16[2048,16,128]{2,0,1:T(8,128)(2,1)S(1)} %get-tuple-element.157) | copy-start | bytes 25165828
  71.9 5.3 %copy-start.7 = (bf16[2048,16,128]{2,0,1:T(8,128)(2,1)}, bf16[2048,16,128]{2,0,1:T(8,128)(2,1)S(1)}, u32[]{:S(2)}) copy-start(bf16[2048,16,128]{2,0,1:T(8,128)(2,1)S(1)} %get-tuple-element.163) | copy-start | bytes 25165828
  79.6 7.1 %copy-start.8 = (bf16[2048,16,128]{2,0,1:T(8,128)(2,1)}, bf16[2048,16,128]{2,0,1:T(8,128)(2,1)S(1)}, u32[]{:S(2)}) copy-start(bf16[2048,16,128]{2,0,1:T(8,128)(2,1)S(1)} %get-tuple-element.168) | copy-start | bytes 25165828
  86.7 14.3 %copy-start.9 = (bf16[2048,16,128]{2,0,1:T(8,128)(2,1)}, bf16[2048,16,128]{2,0,1:T(8,128)(2,1)S(1)}, u32[]{:S(2)}) copy-start(bf16[2048,16,128]{2,0,1:T(8,128)(2,1)S(1)} %get-tuple-element.172) | copy-start | bytes 25165828
  176.7 9.8 %copy-start.2 = (bf16[2048,128]{1,0:T(8,128)(2,1)S(1)}, bf16[2048,128]{1,0:T(8,128)(2,1)}, u32[]{:S(2)}) copy-start(bf16[2048,128]{1,0:T(8,128)(2,1)} %param.8) | copy-start | bytes 1572868
  191.4 20.5 %all-to-all-start = ((bf16[8,2,16384]{2,1,0:T(2,128)(2,1)}), bf16[8,2,16384]{2,1,0:T(2,128)(2,1)}, u32[]{:S(2)}, u32[]{:S(2)}) async-start(bf16[8,2,16384]{2,1,0:T(2,128)(2,1)} %reshape.110), calls=%async_computation | async-start | bytes 1048576 | tf_op jit(solution)/shard_map/all_to_all | solution.py:85
  256.3 10.6 %copy-start.1 = (bf16[2048,128]{1,0:T(8,128)(2,1)S(1)}, bf16[2048,128]{1,0:T(8,128)(2,1)}, u32[]{:S(2)}) copy-start(bf16[2048,128]{1,0:T(8,128)(2,1)} %param.12) | copy-start | bytes 1572868
  263.2 30.1 %all-to-all-start.2 = ((bf16[256,8,255]{2,0,1:T(8,128)(2,1)}), bf16[256,8,255]{2,0,1:T(8,128)(2,1)S(1)}, u32[]{:S(2)}, u32[]{:S(2)}) async-start(bf16[256,8,255]{2,0,1:T(8,128)(2,1)} %copy.106), calls=%async_computation.2 | async-start | bytes 2097152 | tf_op jit(solution)/shard_map/all_to_all | solution.py:109
  335.5 14.1 %copy-start.5 = (bf16[2048,16,1]{1,0,2:T(8,128)(2,1)S(1)}, bf16[2048,16,1]{1,0,2:T(8,128)(2,1)}, u32[]{:S(2)}) copy-start(bf16[2048,16,1]{1,0,2:T(8,128)(2,1)} %get-tuple-element.182) | copy-start | bytes 196612
  341.4 3.2 copy-start.10
  341.4 5.8 %copy-start.11 = (bf16[2048,16,128]{2,0,1:T(8,128)(2,1)}, bf16[2048,16,128]{2,0,1:T(8,128)(2,1)S(1)}, u32[]{:S(2)}) copy-start(bf16[2048,16,128]{2,0,1:T(8,128)(2,1)S(1)} %get-tuple-element.14) | copy-start | bytes 25165828
  341.4 8.2 %copy-start.12 = (bf16[2048,16,128]{2,0,1:T(8,128)(2,1)}, bf16[2048,16,128]{2,0,1:T(8,128)(2,1)S(1)}, u32[]{:S(2)}) copy-start(bf16[2048,16,128]{2,0,1:T(8,128)(2,1)S(1)} %get-tuple-element.15) | copy-start | bytes 25165828
  341.4 17.4 %copy-start.4 = (bf16[2048,16,1]{1,0,2:T(8,128)(2,1)S(1)}, bf16[2048,16,1]{1,0,2:T(8,128)(2,1)}, u32[]{:S(2)}) copy-start(bf16[2048,16,1]{1,0,2:T(8,128)(2,1)} %get-tuple-element.177) | copy-start | bytes 196612
  414.5 10.1 %copy-start.3 = (bf16[2048,128]{1,0:T(8,128)(2,1)S(1)}, bf16[2048,128]{1,0:T(8,128)(2,1)}, u32[]{:S(2)}) copy-start(bf16[2048,128]{1,0:T(8,128)(2,1)} %param.13) | copy-start | bytes 1572868
where the time goes:
time: 436 us; the launch traced here: 429 us
  matrix products  201 us (46%)
  other arithmetic  97.6 us (22%)
  local copies, waits for them, and re-layouts  78 us (18%)
  waiting for transfers between devices  34.1 us (8%)
  starting transfers between devices  17.4 us (4%)
    dot_general x16, matrix products, depthwise(): jnp.einsum('cgl,cg->cl', stacked, kernel_taps[:, first:last], preferred_e...  151 us
    unnamed x91, other arithmetic  67.5 us
    unnamed x49, local copies, waits for them, and re-layouts  62 us
    dot_general x18, matrix products, contract(): return jnp.einsum(form, left, right, precision=lax.Precision.HIGHEST)  50 us
    all_to_all x1, waiting for transfers between devices, on_device(): lax.all_to_all(windows, ('tok', 'sec'), split_axis=1, concat_axis=0, tile...  23.6 us
    another operation x8, other arithmetic, depthwise(): jnp.stack([padded[:, tap_count - 1 - k:tap_count - 1 - k + length] for k...  19.8 us
    all_to_all x1, waiting for transfers between devices, on_device(): lax.all_to_all(mixed_one[:, None, :], ('tok', 'sec'), split_axis=0, conca...  10.4 us
  transfers between devices with their start and end apart: 4, of which 2 were waited for; matrix products, arithmetic and copies ran while one was open for 43% of the time, Pallas kernels for 0%

commit v1 on v0

--- a/solution.py
+++ b/solution.py
@@ -3,6 +3,12 @@
 import jax.numpy as jnp
 from jax import lax
 from jax.sharding import PartitionSpec as P
+
+
+def stacked_exchange(x, axis, split, join):
+    cells = jnp.split(x, lax.axis_size(axis), axis=split)
+    incoming = lax.all_to_all(jnp.stack(cells), axis, 0, 0)
+    return jnp.concatenate(incoming, axis=join)
 
 
 def passed_along(array, axis, by):
@@ -106,9 +112,9 @@
         axis=1,
     )
     windows = jnp.concatenate([tail_rows, long_blocks], axis=2)
-    padded = lax.all_to_all(
-        windows, ("tok", "sec"), split_axis=1, concat_axis=0, tiled=True
-    ).reshape(channels, block_len + rim_width)
+    padded = stacked_exchange(windows, ("tok", "sec"), 1, 0).reshape(
+        channels, block_len + rim_width
+    )
     second_conv = depthwise(padded, taps_two)
     return (second_conv * gate_two).astype(jnp.bfloat16)
 

time: 436 us -> 441 us (1.011)
  local copies, waits for them, and re-layouts: 78 us -> 83.9 us
    unnamed x49 -> x56, local copies, waits for them, and re-layouts: 62 us -> 66.5 us
  transfers between devices with their start and end apart: 4 -> 4, of which waited for: 2 -> 2; matrix products, arithmetic and copies ran while one was open for 43% -> 42% of each run, Pallas kernels for 0% -> 0%
where the time goes in v1:
time: 441 us; the launch traced here: 434 us
  matrix products  201 us (46%)
  other arithmetic  97.2 us (22%)
  local copies, waits for them, and re-layouts  83.9 us (19%)
  waiting for transfers between devices  34.1 us (8%)
  starting transfers between devices  17.4 us (4%)
    dot_general x16, matrix products, depthwise(): jnp.einsum('cgl,cg->cl', stacked, kernel_taps[:, first:last], preferred_e...  151 us
    unnamed x91, other arithmetic  67.4 us
    unnamed x56, local copies, waits for them, and re-layouts  66.5 us
    dot_general x18, matrix products, contract(): return jnp.einsum(form, left, right, precision=lax.Precision.HIGHEST)  50 us
    all_to_all x1, waiting for transfers between devices, stacked_exchange(): incoming = lax.all_to_all(jnp.stack(cells), axis, 0, 0)  23.6 us
    another operation x8, other arithmetic, depthwise(): jnp.stack([padded[:, tap_count - 1 - k:tap_count - 1 - k + length] for k...  19.7 us
    all_to_all x1, waiting for transfers between devices, on_device(): lax.all_to_all(mixed_one[:, None, :], ('tok', 'sec'), split_axis=0, conca...  10.4 us
  transfers between devices with their start and end apart: 4, of which 2 were waited for; matrix products, arithmetic and copies ran while one was open for 42% of the time, Pallas kernels for 0%

profile of v1, /device:TPU:0, one launch (start us, length us, event | category | flops | bytes accessed | tf_op | source)
XLA Modules:
  0.0 434.0 jit_solution(11005912190128471713)
XLA Ops:
  7.9 6.1 %all-to-all-start.1 = ((bf16[8,2,16384]{2,1,0:T(2,128)(2,1)}), bf16[8,2,16384]{2,1,0:T(2,128)(2,1)S(1)}, u32[]{:S(2)}, u32[]{:S(2)}) async-start(bf16[8,2,16384]{2,1,0:T(2,128)(2,1)} %reshape.107), calls=%async_computation.1 | async-start | bytes 1048576 | tf_op jit(solution)/shard_map/all_to_all | solution.py:85
  14.1 5.7 %slice_bitcast_fusion.142 = (bf16[2048,16,1]{1,0,2:T(8,128)(2,1)S(1)}, bf16[2048,16,1]{1,0,2:T(8,128)(2,1)}, bf16[2048,16,1]{1,0,2:T(8,128)(2,1)}, bf16[2048,16,...) fusion(bf16[2048,128]{1,0:T(8,128)(2,1)} %param.9), kind=kLoop, calls=%fused_computation.1021 | loop fusion | bytes 1048576 | tf_op jit(solution)/shard_map/slice | solution.py:32
  27.7 3.2 copy-done.13
  31.0 3.7 constant_dynamic-update-slice_fusion.16
  50.5 3.0 constant_dynamic-update-slice_fusion
  59.8 3.2 constant_dynamic-update-slice_fusion.32
  68.8 2.8 constant_dynamic-update-slice_fusion.48
  110.4 8.7 %fusion.16 = f32[2048,1,128]{2,1,0:T(1,128)S(1)} fusion(bf16[2048,16,128]{2,0,1:T(8,128)(2,1)} %constant_dynamic-update-slice_fusion.112, bf16[2048,16,1]{1,0,2:T(8,128)(2,1)S(1)} %get-tuple-element.199), kind=kOutput, calls=%fused_computation.268 | convolution fusion | flops 8388608 | bytes 9502720 | tf_op jit(solution)/shard_map/cgl,cg->cl/dot_general | solution.py:31
  119.1 8.7 %fusion.18 = f32[2048,1,128]{2,1,0:T(1,128)S(1)} fusion(bf16[2048,16,128]{2,0,1:T(8,128)(2,1)} %get-tuple-element.183, bf16[2048,16,1]{1,0,2:T(8,128)(2,1)S(1)} %get-tuple-element.200), kind=kOutput, calls=%fused_computation.270 | convolution fusion | flops 8388608 | bytes 9502720 | tf_op jit(solution)/shard_map/cgl,cg->cl/dot_general | solution.py:31
  127.8 9.0 %fusion.20 = f32[2048,1,128]{2,1,0:T(1,128)S(1)} fusion(bf16[2048,16,128]{2,0,1:T(8,128)(2,1)} %copy-done.9, bf16[2048,16,1]{1,0,2:T(8,128)(2,1)} %get-tuple-element.194), kind=kOutput, calls=%fused_computation.272 | convolution fusion | flops 8388608 | bytes 9502720 | tf_op jit(solution)/shard_map/cgl,cg->cl/dot_general | solution.py:31
  136.8 9.7 %fusion.22 = f32[2048,1,128]{2,1,0:T(1,128)} fusion(bf16[2048,16,128]{2,0,1:T(8,128)(2,1)} %copy-done.8, bf16[2048,16,1]{1,0,2:T(8,128)(2,1)} %get-tuple-element.195), kind=kOutput, calls=%fused_computation.274 | convolution fusion | flops 8388608 | bytes 9502720 | tf_op jit(solution)/shard_map/cgl,cg->cl/dot_general | solution.py:31
  146.5 10.2 %fusion.24 = f32[2048,1,128]{2,1,0:T(1,128)} fusion(bf16[2048,16,128]{2,0,1:T(8,128)(2,1)} %copy-done.7, bf16[2048,16,1]{1,0,2:T(8,128)(2,1)} %get-tuple-element.196), kind=kOutput, calls=%fused_computation.276 | convolution fusion | flops 8388608 | bytes 9502720 | tf_op jit(solution)/shard_map/cgl,cg->cl/dot_general | solution.py:31
  156.7 9.8 %fusion.26 = f32[2048,1,128]{2,1,0:T(1,128)} fusion(bf16[2048,16,128]{2,0,1:T(8,128)(2,1)} %copy-done.6, bf16[2048,16,1]{1,0,2:T(8,128)(2,1)} %get-tuple-element.197), kind=kOutput, calls=%fused_computation.278 | convolution fusion | flops 8388608 | bytes 9502720 | tf_op jit(solution)/shard_map/cgl,cg->cl/dot_general | solution.py:31
  166.5 9.9 %fusion.30 = f32[2048,1,128]{2,1,0:T(1,128)} fusion(bf16[2048,16,128]{2,0,1:T(8,128)(2,1)} %get-tuple-element.157, bf16[2048,16,1]{1,0,2:T(8,128)(2,1)S(1)} %get-tuple-element.198), kind=kOutput, calls=%fused_computation.282 | convolution fusion | flops 8388608 | bytes 9502720 | tf_op jit(solution)/shard_map/cgl,cg->cl/dot_general | solution.py:31
  176.3 9.8 %fusion.28 = f32[2048,1,128]{2,1,0:T(1,128)} fusion(bf16[2048,16,128]{2,0,1:T(8,128)(2,1)} %get-tuple-element.149, bf16[2048,16,1]{1,0,2:T(8,128)(2,1)S(1)} %get-tuple-element.193), kind=kOutput, calls=%fused_computation.280 | convolution fusion | flops 8388608 | bytes 9502720 | tf_op jit(solution)/shard_map/cgl,cg->cl/dot_general | solution.py:31
  186.1 2.9 fusion.111
  190.9 5.1 %all-to-all-start = ((bf16[8,2,16384]{2,1,0:T(2,128)(2,1)}), bf16[8,2,16384]{2,1,0:T(2,128)(2,1)}, u32[]{:S(2)}, u32[]{:S(2)}) async-start(bf16[8,2,16384]{2,1,0:T(2,128)(2,1)} %reshape.105), calls=%async_computation | async-start | bytes 1048576 | tf_op jit(solution)/shard_map/all_to_all | solution.py:91
  198.6 2.4 fusion.367
  201.0 10.4 %all-to-all-done = bf16[8,2,16384]{2,1,0:T(2,128)(2,1)} async-done(((bf16[8,2,16384]{2,1,0:T(2,128)(2,1)}), bf16[8,2,16384]{2,1,0:T(2,128)(2,1)}, u32[]{:S(2)}, u32[]{:S(2)}) %all-to-all-start) | async-done | bytes 524320 | tf_op jit(solution)/shard_map/all_to_all | solution.py:91
  211.4 2.6 reshape.106
  215.3 3.5 add_bitcast_fusion
  218.8 2.6 fusion.47
  221.4 2.6 fusion.45
  224.0 2.6 fusion.55
  226.6 2.7 fusion.53
  229.4 2.7 fusion.67
  232.1 2.7 fusion.70
  234.8 2.7 fusion.61
  237.5 3.3 multiply_subtract_fusion.1
  240.9 3.6 fusion.34
  244.4 3.6 fusion.32
  248.1 4.0 fusion.73
  252.1 3.8 multiply_subtract_fusion
  258.1 2.6 fusion.91
  268.8 3.7 all-to-all-start.2
  272.5 2.7 slice_bitcast_fusion.134
  275.2 23.6 %all-to-all-done.2 = bf16[8,256,1,255]{3,1,2,0:T(8,128)(2,1)S(1)} async-done(((bf16[8,256,1,255]{3,1,2,0:T(8,128)(2,1)}), bf16[8,256,1,255]{3,1,2,0:T(8,128)(2,1)S(1)}, u32[]{:S(2)}, u32[]{:S(2)}) %all-to-all-start.2) | async-done | bytes 1044512 | tf_op jit(solution)/shard_map/all_to_all | solution.py:10
  298.8 2.7 constant_dynamic-update-slice_fusion.167
  301.6 3.0 constant_dynamic-update-slice_fusion.166
  304.6 3.0 constant_dynamic-update-slice_fusion.165
  307.6 3.0 constant_dynamic-update-slice_fusion.164
  310.6 3.0 constant_dynamic-update-slice_fusion.163
  313.6 3.1 constant_dynamic-update-slice_fusion.162
  316.7 3.0 constant_dynamic-update-slice_fusion.161
  319.7 3.0 constant_dynamic-update-slice_fusion.160
  322.7 3.1 constant_dynamic-update-slice_fusion.159
  325.8 3.2 constant_dynamic-update-slice_fusion.158
  329.0 3.0 constant_dynamic-update-slice_fusion.157
  332.0 3.0 constant_dynamic-update-slice_fusion.156
  335.0 3.0 constant_dynamic-update-slice_fusion.155
  338.0 3.0 constant_dynamic-update-slice_fusion.154
  341.0 3.0 constant_dynamic-update-slice_fusion.153
  344.0 2.8 constant_dynamic-update-slice_fusion.152
  346.8 3.2 copy-done.10
  350.1 2.6 copy-done.11
  355.1 9.1 %fusion.14 = f32[2048,1,128]{2,1,0:T(1,128)S(1)} fusion(bf16[2048,16,128]{2,0,1:T(8,128)(2,1)} %get-tuple-element.20, bf16[2048,16,1]{1,0,2:T(8,128)(2,1)S(1)} %copy-done.5), kind=kOutput, calls=%fused_computation.266 | convolution fusion | flops 8388608 | bytes 9502720 | tf_op jit(solution)/shard_map/cgl,cg->cl/dot_general | solution.py:31
  364.2 8.7 %fusion.12 = f32[2048,1,128]{2,1,0:T(1,128)S(1)} fusion(bf16[2048,16,128]{2,0,1:T(8,128)(2,1)} %copy-done.10, bf16[2048,16,1]{1,0,2:T(8,128)(2,1)S(1)} %copy-done.4), kind=kOutput, calls=%fused_computation.264 | convolution fusion | flops 8388608 | bytes 9502720 | tf_op jit(solution)/shard_map/cgl,cg->cl/dot_general | solution.py:31
  372.9 8.9 %fusion.10 = f32[2048,1,128]{2,1,0:T(1,128)S(1)} fusion(bf16[2048,16,128]{2,0,1:T(8,128)(2,1)} %get-tuple-element.19, bf16[2048,16,1]{1,0,2:T(8,128)(2,1)S(1)} %get-tuple-element.189), kind=kOutput, calls=%fused_computation.262 | convolution fusion | flops 8388608 | bytes 9502720 | tf_op jit(solution)/shard_map/cgl,cg->cl/dot_general | solution.py:31
  381.8 8.8 %fusion.8 = f32[2048,1,128]{2,1,0:T(1,128)S(1)} fusion(bf16[2048,16,128]{2,0,1:T(8,128)(2,1)} %get-tuple-element.18, bf16[2048,16,1]{1,0,2:T(8,128)(2,1)} %get-tuple-element.188), kind=kOutput, calls=%fused_computation.260 | convolution fusion | flops 8388608 | bytes 9502720 | tf_op jit(solution)/shard_map/cgl,cg->cl/dot_general | solution.py:31
  390.6 9.9 %fusion.6 = f32[2048,1,128]{2,1,0:T(1,128)} fusion(bf16[2048,16,128]{2,0,1:T(8,128)(2,1)} %get-tuple-element.17, bf16[2048,16,1]{1,0,2:T(8,128)(2,1)} %get-tuple-element.187), kind=kOutput, calls=%fused_computation.258 | convolution fusion | flops 8388608 | bytes 9502720 | tf_op jit(solution)/shard_map/cgl,cg->cl/dot_general | solution.py:31
  400.5 9.7 %fusion.4 = f32[2048,1,128]{2,1,0:T(1,128)} fusion(bf16[2048,16,128]{2,0,1:T(8,128)(2,1)} %get-tuple-element.16, bf16[2048,16,1]{1,0,2:T(8,128)(2,1)} %get-tuple-element.186), kind=kOutput, calls=%fused_computation.256 | convolution fusion | flops 8388608 | bytes 9502720 | tf_op jit(solution)/shard_map/cgl,cg->cl/dot_general | solution.py:31
  410.3 9.7 %fusion.2 = f32[2048,1,128]{2,1,0:T(1,128)} fusion(bf16[2048,16,128]{2,0,1:T(8,128)(2,1)} %copy-done.12, bf16[2048,16,1]{1,0,2:T(8,128)(2,1)S(1)} %get-tuple-element.192), kind=kOutput, calls=%fused_computation.254 | convolution fusion | flops 8388608 | bytes 9502720 | tf_op jit(solution)/shard_map/cgl,cg->cl/dot_general | solution.py:31
  419.9 10.0 %fusion = f32[2048,1,128]{2,1,0:T(1,128)} fusion(bf16[2048,16,128]{2,0,1:T(8,128)(2,1)} %copy-done.11, bf16[2048,16,1]{1,0,2:T(8,128)(2,1)} %get-tuple-element.191), kind=kOutput, calls=%fused_computation.252 | convolution fusion | flops 8388608 | bytes 9502720 | tf_op jit(solution)/shard_map/cgl,cg->cl/dot_general | solution.py:31
  430.0 3.6 multiply_convert_fusion
  (148 shorter events, 100.8 us)
Async XLA Ops:
  0.0 19.8 %copy-start = (bf16[2048,128]{1,0:T(8,128)(2,1)S(1)}, bf16[2048,128]{1,0:T(8,128)(2,1)}, u32[]{:S(2)}) copy-start(bf16[2048,128]{1,0:T(8,128)(2,1)} %param.7) | copy-start | bytes 1572868
  2.1 17.6 %collective-permute-start = (bf16[2048,127]{1,0:T(8,128)(2,1)}, bf16[2048,127]{1,0:T(8,128)(2,1)S(1)}, u32[]{:S(2)}, u32[]{:S(2)}) collective-permute-start(bf16[2048,127]{1,0:T(8,128)(2,1)} %slice.819), channel_id=1, source_target_pairs={{0,2},{2,4},{4,6},{6,8},{8,10},{10,12},{12,14},{1,3},{3,5},{5,7},{... | collective-permute-start | bytes 1560584 | tf_op jit(solution)/shard_map/ppermute | solution.py:17
  7.9 183.0 %all-to-all-start.1 = ((bf16[8,2,16384]{2,1,0:T(2,128)(2,1)}), bf16[8,2,16384]{2,1,0:T(2,128)(2,1)S(1)}, u32[]{:S(2)}, u32[]{:S(2)}) async-start(bf16[8,2,16384]{2,1,0:T(2,128)(2,1)} %reshape.107), calls=%async_computation.1 | async-start | bytes 1048576 | tf_op jit(solution)/shard_map/all_to_all | solution.py:85
  27.7 3.2 copy-start.13
  63.0 5.3 %copy-start.6 = (bf16[2048,16,128]{2,0,1:T(8,128)(2,1)}, bf16[2048,16,128]{2,0,1:T(8,128)(2,1)S(1)}, u32[]{:S(2)}) copy-start(bf16[2048,16,128]{2,0,1:T(8,128)(2,1)S(1)} %get-tuple-element.165) | copy-start | bytes 25165828
  71.6 5.3 %copy-start.7 = (bf16[2048,16,128]{2,0,1:T(8,128)(2,1)}, bf16[2048,16,128]{2,0,1:T(8,128)(2,1)S(1)}, u32[]{:S(2)}) copy-start(bf16[2048,16,128]{2,0,1:T(8,128)(2,1)S(1)} %get-tuple-element.171) | copy-start | bytes 25165828
  79.2 7.1 %copy-start.8 = (bf16[2048,16,128]{2,0,1:T(8,128)(2,1)}, bf16[2048,16,128]{2,0,1:T(8,128)(2,1)S(1)}, u32[]{:S(2)}) copy-start(bf16[2048,16,128]{2,0,1:T(8,128)(2,1)S(1)} %get-tuple-element.176) | copy-start | bytes 25165828
  86.4 14.3 %copy-start.9 = (bf16[2048,16,128]{2,0,1:T(8,128)(2,1)}, bf16[2048,16,128]{2,0,1:T(8,128)(2,1)S(1)}, u32[]{:S(2)}) copy-start(bf16[2048,16,128]{2,0,1:T(8,128)(2,1)S(1)} %get-tuple-element.180) | copy-start | bytes 25165828
  176.3 9.8 %copy-start.2 = (bf16[2048,128]{1,0:T(8,128)(2,1)S(1)}, bf16[2048,128]{1,0:T(8,128)(2,1)}, u32[]{:S(2)}) copy-start(bf16[2048,128]{1,0:T(8,128)(2,1)} %param.8) | copy-start | bytes 1572868
  190.9 20.5 %all-to-all-start = ((bf16[8,2,16384]{2,1,0:T(2,128)(2,1)}), bf16[8,2,16384]{2,1,0:T(2,128)(2,1)}, u32[]{:S(2)}, u32[]{:S(2)}) async-start(bf16[8,2,16384]{2,1,0:T(2,128)(2,1)} %reshape.105), calls=%async_computation | async-start | bytes 1048576 | tf_op jit(solution)/shard_map/all_to_all | solution.py:91
  258.1 14.5 %copy-start.1 = (bf16[2048,128]{1,0:T(8,128)(2,1)S(1)}, bf16[2048,128]{1,0:T(8,128)(2,1)}, u32[]{:S(2)}) copy-start(bf16[2048,128]{1,0:T(8,128)(2,1)} %param.12) | copy-start | bytes 1572868
  268.8 30.1 %all-to-all-start.2 = ((bf16[8,256,1,255]{3,1,2,0:T(8,128)(2,1)}), bf16[8,256,1,255]{3,1,2,0:T(8,128)(2,1)S(1)}, u32[]{:S(2)}, u32[]{:S(2)}) async-start(bf16[8,256,1,255]{3,1,2,0:T(8,128)(2,1)} %constant_dynamic-update-slice_fusion.128), calls=%async_computation.2 | async-start | bytes 2097152 | tf_op jit(solution)/shard_map/all_to_all | solution.py:10
  341.0 14.1 %copy-start.5 = (bf16[2048,16,1]{1,0,2:T(8,128)(2,1)S(1)}, bf16[2048,16,1]{1,0,2:T(8,128)(2,1)}, u32[]{:S(2)}) copy-start(bf16[2048,16,1]{1,0,2:T(8,128)(2,1)} %get-tuple-element.190) | copy-start | bytes 196612
  346.8 3.2 copy-start.10
  346.8 5.8 %copy-start.11 = (bf16[2048,16,128]{2,0,1:T(8,128)(2,1)}, bf16[2048,16,128]{2,0,1:T(8,128)(2,1)S(1)}, u32[]{:S(2)}) copy-start(bf16[2048,16,128]{2,0,1:T(8,128)(2,1)S(1)} %get-tuple-element.14) | copy-start | bytes 25165828
  346.8 8.3 %copy-start.12 = (bf16[2048,16,128]{2,0,1:T(8,128)(2,1)}, bf16[2048,16,128]{2,0,1:T(8,128)(2,1)S(1)}, u32[]{:S(2)}) copy-start(bf16[2048,16,128]{2,0,1:T(8,128)(2,1)S(1)} %get-tuple-element.15) | copy-start | bytes 25165828
  346.8 17.4 %copy-start.4 = (bf16[2048,16,1]{1,0,2:T(8,128)(2,1)S(1)}, bf16[2048,16,1]{1,0,2:T(8,128)(2,1)}, u32[]{:S(2)}) copy-start(bf16[2048,16,1]{1,0,2:T(8,128)(2,1)} %get-tuple-element.185) | copy-start | bytes 196612
  419.9 10.1 %copy-start.3 = (bf16[2048,128]{1,0:T(8,128)(2,1)S(1)}, bf16[2048,128]{1,0:T(8,128)(2,1)}, u32[]{:S(2)}) copy-start(bf16[2048,128]{1,0:T(8,128)(2,1)} %param.13) | copy-start | bytes 1572868
